TPU v7x, 256 devices: a whole 4x4x8 slice. The times are simulated.
256 devices in a mesh: row: 16 (over y_lo, x, core), col: 16 (over y_hi, z).
Axes of the slice: x: 4, y: 4 (y_hi: 2, y_lo: 2; y = y_hi * 2 + y_lo), z: 8, core: 2. Of those that a mesh axis runs over, the one named last changes fastest.
Arguments:
- field: bfloat16 [64, 64, 32, 512], P('row', 'col'), may hold values from -6 to 6
- near_kernel: bfloat16 [9, 2, 2, 256, 256], replicated, may hold values from -0.09375 to 0.09375
- contact: int32 [64, 64, 9], P('row', 'col'), may hold values from 0 to 1
- pillar_shift: int32 [64, 64, 2], P('row', 'col'), may hold values from 0 to 15
- wave_index: int32 [2048, 2], replicated, may hold values from -32 to 31
- wave_form: bfloat16 [2048, 2, 256], replicated, may hold values from -0.25 to 0.25
- wave_weight: float32 [2048], replicated, may hold values from 0.5 to 4
Outputs:
- applied: float32 [64, 64, 32, 512], P('row', 'col')
All inputs are finite; a program needn't handle non-finite values.
Results may differ from a plain program's by a relative error of at most 0.0038.
Values may be sent and summed in bfloat16 or wider, within the bound.
A program may use at most 128 MiB of HBM per device.

v0:
```python
import math
import jax
import jax.numpy as jnp
from jax import lax
from jax.sharding import PartitionSpec as P

Q = 16
bloch_row = 0.3
bloch_col = 0.17


def extended(cells, sides, width):
    for axis, dim in sides:
        count = lax.axis_size(axis)
        head = lax.slice_in_dim(cells, 0, width, axis=dim)
        tail = lax.slice_in_dim(cells, cells.shape[dim] - width, cells.shape[dim], axis=dim)
        cells = jnp.concatenate(
            [
                lax.ppermute(tail, axis, [(i, (i + 1) % count) for i in range(count)]),
                cells,
                lax.ppermute(head, axis, [((i + 1) % count, i) for i in range(count)]),
            ],
            axis=dim,
        )
    return cells


def realify(real_part, imag_part):
    upper = jnp.concatenate([real_part.T, imag_part.T], axis=1)
    lower = jnp.concatenate([-imag_part.T, real_part.T], axis=1)
    return jnp.concatenate([upper, lower], axis=0)


def wave_angle(wave_index, fine_row, fine_col, row_mod, col_mod):
    order_row = wave_index[:, 0:1]
    order_col = wave_index[:, 1:2]
    turn_row = jnp.mod(order_row * fine_row[None, :], row_mod).astype(jnp.float32) / row_mod
    turn_col = jnp.mod(order_col * fine_col[None, :], col_mod).astype(jnp.float32) / col_mod
    drift = (
        bloch_row * fine_row.astype(jnp.float32) / row_mod
        + bloch_col * fine_col.astype(jnp.float32) / col_mod
    )
    return 2.0 * math.pi * (turn_row + turn_col + drift[None, :])


def local(field, near_kernel, contact, pillar_shift, wave_index, wave_form, wave_weight):
    rows_here = field.shape[0]
    cols_here = field.shape[1]
    sources = field.shape[2]
    width = field.shape[3]
    waves = wave_form.shape[0]
    n_row = lax.axis_size("row")
    n_col = lax.axis_size("col")
    rows_total = rows_here * n_row
    cols_total = cols_here * n_col
    row_mod = Q * rows_total
    col_mod = Q * cols_total
    wave_matrix = realify(wave_form[:, 0], wave_form[:, 1])
    padded = extended(field, (("row", 0), ("col", 1)), 1)
    global_row = lax.axis_index("row") * rows_here + jnp.arange(rows_here, dtype=jnp.int32)
    global_col = lax.axis_index("col") * cols_here + jnp.arange(cols_here, dtype=jnp.int32)
    fine_row = (Q * global_row[:, None] + pillar_shift[:, :, 0]).reshape(-1)
    fine_col = (Q * global_col[None, :] + pillar_shift[:, :, 1]).reshape(-1)
    angles = wave_angle(wave_index, fine_row, fine_col, row_mod, col_mod)
    cos_all = jnp.cos(angles).T
    sin_all = jnp.sin(angles).T
    projected = jnp.dot(field.reshape(-1, width), wave_matrix, preferred_element_type=jnp.float32)
    projected = projected.reshape(rows_here * cols_here, sources, 2, waves)
    hi = lax.Precision.HIGHEST
    coeff_real = jnp.einsum("pw,psw->sw", cos_all, projected[:, :, 0], precision=hi) - jnp.einsum(
        "pw,psw->sw", sin_all, projected[:, :, 1], precision=hi
    )
    coeff_imag = jnp.einsum("pw,psw->sw", cos_all, projected[:, :, 1], precision=hi) + jnp.einsum(
        "pw,psw->sw", sin_all, projected[:, :, 0], precision=hi
    )
    partial_coeff = jnp.stack([coeff_real, coeff_imag], axis=1)
    near = jnp.zeros((rows_here, cols_here, sources, width), jnp.float32)
    for offset in range(9):
        step_row = offset // 3 - 1
        step_col = offset % 3 - 1
        block = padded[
            1 + step_row : 1 + step_row + rows_here, 1 + step_col : 1 + step_col + cols_here
        ]
        block = block.reshape(-1, width)
        for variant in range(near_kernel.shape[1]):
            near_mat = realify(near_kernel[offset, variant, 0], near_kernel[offset, variant, 1])
            product = jnp.dot(block, near_mat, preferred_element_type=jnp.float32).reshape(
                rows_here, cols_here, sources, width
            )
            chosen = (contact[:, :, offset] == variant)[:, :, None, None]
            near = near + jnp.where(chosen, product, jnp.float32(0.0))
    far_scale = math.sqrt(width // 2 / (waves * rows_total * cols_total))
    owned = lax.psum_scatter(partial_coeff, ("row", "col"), scatter_dimension=2, tiled=True)
    owner = lax.axis_index("row") * n_col + lax.axis_index("col")
    count = owned.shape[2]
    scales = far_scale * lax.dynamic_slice_in_dim(wave_weight, owner * owned.shape[2], count, 0)
    weighted = (scales[None, None, :] * owned).astype(jnp.bfloat16)
    add_weighted = lax.all_gather(weighted, ("row", "col"), axis=2, tiled=True)
    count = add_weighted.shape[2]
    cos_part = cos_all[:, None, :]
    sin_part = sin_all[:, None, :]
    weight_real = add_weighted[:, 0].astype(jnp.float32)[None]
    weight_imag = add_weighted[:, 1].astype(jnp.float32)[None]
    spread_real = cos_part * weight_real + sin_part * weight_imag
    spread_imag = cos_part * weight_imag - sin_part * weight_real
    spread = (
        jnp.concatenate([spread_real, spread_imag], axis=-1)
        .astype(jnp.bfloat16)
        .reshape(-1, 2 * count)
    )
    columns = jnp.concatenate(
        [
            lax.slice_in_dim(wave_matrix, 0, count, axis=1),
            lax.dynamic_slice_in_dim(wave_matrix, waves, count, 1),
        ],
        axis=1,
    )
    far = lax.dot_general(
        spread, columns, (((1,), (1,)), ((), ())), preferred_element_type=jnp.float32
    )
    return near + far.reshape(rows_here, cols_here, sources, width)


def solution(mesh):
    placed = (
        P("row", "col", None, None),
        P(),
        P("row", "col", None),
        P("row", "col", None),
        P(),
        P(),
        P(),
    )
    return jax.shard_map(
        local, mesh=mesh, in_specs=placed, out_specs=P("row", "col", None, None), check_vma=False
    )
```

profile of v0, /device:TPU:0, one launch (start us, length us, event | category | flops | bytes accessed | tf_op | source)
XLA Modules:
  0.0 1004.8 jit_solution(13671285341603411900)
XLA Ops:
  6.5 6.5 fusion.183
  13.0 5.8 copy.195
  18.8 2.6 copy.196
  22.5 7.4 convolution_bitcast_fusion
  29.9 8.9 copy.148
  38.8 11.8 %reshape.487 = f32[16,32,2,2048]{3,2,1,0:T(2,128)} reshape(f32[512,4096]{1,0:T(8,128)} %copy.148) | data formatting | bytes 16777216 | tf_op jit(solution)/shard_map/reshape | solution.py:68
  50.6 12.1 %fusion.180 = (f32[16,32,1,2048]{3,2,1,0:T(1,128)}, f32[16,32,1,2048]{3,2,1,0:T(1,128)}) fusion(f32[16,32,2,2048]{3,2,1,0:T(2,128)} %reshape.487), kind=kLoop, calls=%fused_computation.305 | loop fusion | bytes 16777216 | tf_op jit(solution)/shard_map/slice | solution.py:71
  64.9 6.9 fusion.6
  72.0 2.2 copy.149
  75.0 3.9 collective-permute-start.1
  78.9 2.7 fusion.181
  81.6 3.0 fusion.182
  84.6 1.7 fusion.178
  86.3 1.7 copy.228
  87.9 1.6 bitcast_negate_fusion.1
  89.5 1.7 copy.226
  91.2 1.6 bitcast_negate_fusion.2
  92.7 1.7 copy.224
  94.4 1.6 bitcast_negate_fusion.3
  95.9 1.7 copy.222
  97.6 1.6 bitcast_negate_fusion.4
  99.2 1.7 copy.220
  100.8 1.6 bitcast_negate_fusion.5
  102.4 1.7 copy.218
  104.1 1.6 bitcast_negate_fusion.6
  105.6 1.7 copy.216
  107.3 1.5 bitcast_negate_fusion.7
  109.6 1.6 bitcast_negate_fusion.9
  115.4 1.7 copy.204
  117.1 1.6 bitcast_negate_fusion.13
  118.6 1.6 copy.202
  120.3 1.6 bitcast_negate_fusion.14
  121.8 1.7 copy.200
  123.5 1.6 bitcast_negate_fusion.15
  127.6 2.0 fusion.156
  129.6 2.6 fusion.83
  132.2 2.6 fusion.75
  142.3 1.7 copy.207
  143.9 1.7 copy.205
  145.6 1.7 copy.203
  147.2 1.7 copy.201
  149.0 1.7 copy.199
  152.1 1.9 compare_reduce_fusion.7
  156.9 6.8 collective-permute-start.3
  163.7 2.4 convolution_select_fusion
  166.1 2.5 convolution_select_fusion.1
  168.6 1.5 convolution_select_fusion.2
  170.1 1.4 convolution_select_fusion.3
  171.6 165.6 %all-reduce.3.cloned.1.call-done = f32[32,2,2048]{0,1,2:T(2,128)} async-done(((f32[32,2,2048]{0,1,2:T(2,128)}), f32[32,2,2048]{0,1,2:T(2,128)}) %all-reduce.3.cloned.1.call-update) | async-done | bytes 524304
  337.9 630.5 %all_gather.3 = bf16[32,2,2048]{0,1,2:T(2,128)(2,1)S(1)} all-gather(bf16[32,2,8]{0,1,2:T(2,128)(2,1)S(1)} %fusion.157), channel_id=1, replica_groups=mesh['row'=16,'col'=16] {'row','col'}, dimensions={2}, use_global_device_ids=true | all-gather | bytes 263168 | tf_op jit(solution)/shard_map/all_gather | solution.py:98
  968.4 2.2 slice_convert_fusion.1
  970.6 1.5 copy.151
  973.2 2.5 add_convert_fusion
  975.7 2.4 fusion
  978.2 1.5 convolution_select_fusion.4
  979.8 1.4 convolution_select_fusion.5
  981.3 1.4 convolution_select_fusion.6
  982.8 1.4 convolution_select_fusion.7
  984.3 1.4 convolution_select_fusion.8
  987.3 1.4 convolution_select_fusion.11
  988.8 1.4 convolution_select_fusion.12
  990.3 1.5 convolution_select_fusion.13
  993.3 1.9 fusion.26
  995.2 2.7 fusion.25
  (196 shorter events, 28.3 us)
Async XLA Ops:
  6.5 330.6 %all-reduce.3.cloned.1.call-start = ((), (), s32[]{:S(2)}) async-start(), calls=%async_computation | async-start | bytes 4194304
  50.6 12.7 %copy-start.57 = (s32[4,4,2]{1,2,0:T(2,128)S(1)}, s32[4,4,2]{1,2,0:T(2,128)}, u32[]{:S(2)}) copy-start(s32[4,4,2]{1,2,0:T(2,128)} %param.10) | copy-start | bytes 388
  50.6 13.6 %copy-start.56 = (s32[2048,2]{0,1:T(2,128)S(1)}, s32[2048,2]{0,1:T(2,128)}, u32[]{:S(2)}) copy-start(s32[2048,2]{0,1:T(2,128)} %param.11) | copy-start | bytes 49156
  64.1 7.8 copy-start.59
  75.0 79.0 %collective-permute-start = (bf16[1,4,32,512]{3,2,1,0:T(8,128)(2,1)}, bf16[1,4,32,512]{3,2,1,0:T(8,128)(2,1)}, u32[]{:S(2)}, u32[]{:S(2)}) collective-permute-start(bf16[1,4,32,512]{3,2,1,0:T(8,128)(2,1)} %get-tuple-element.89), channel_id=1, source_target_pairs={{0,16},{16,32},{32,48},{48,64},{64,80},{80,96},{96,112},{112,128},... | collective-permute-start | bytes 393224 | tf_op jit(solution)/shard_map/ppermute | solution.py:19
  75.0 80.1 %collective-permute-start.1 = (bf16[1,4,32,512]{3,2,1,0:T(8,128)(2,1)}, bf16[1,4,32,512]{3,2,1,0:T(8,128)(2,1)}, u32[]{:S(2)}, u32[]{:S(2)}) collective-permute-start(bf16[1,4,32,512]{3,2,1,0:T(8,128)(2,1)} %get-tuple-element.88), channel_id=1, source_target_pairs={{16,0},{32,16},{48,32},{64,48},{80,64},{96,80},{112,96},{128,112},... | collective-permute-start | bytes 393224 | tf_op jit(solution)/shard_map/ppermute | solution.py:21
  111.2 13.8 %copy-start.18 = (bf16[1,1,1,256,256]{3,4,2,1,0:T(8,128)(2,1)}, bf16[1,1,1,256,256]{3,4,2,1,0:T(8,128)(2,1)S(1)}, u32[]{:S(2)}) copy-start(bf16[1,1,1,256,256]{3,4,2,1,0:T(8,128)(2,1)S(1)} %copy.210) | copy-start | bytes 393220
  114.7 12.1 %copy-start.14 = (bf16[1,1,1,256,256]{3,4,2,1,0:T(8,128)(2,1)}, bf16[1,1,1,256,256]{3,4,2,1,0:T(8,128)(2,1)S(1)}, u32[]{:S(2)}) copy-start(bf16[1,1,1,256,256]{3,4,2,1,0:T(8,128)(2,1)S(1)} %copy.206) | copy-start | bytes 393220
  132.2 20.0 %copy-start.10 = (s32[4,4,9]{2,1,0:T(4,128)S(1)}, s32[4,4,9]{2,1,0:T(4,128)}, u32[]{:S(2)}) copy-start(s32[4,4,9]{2,1,0:T(4,128)} %param.9) | copy-start | bytes 1732
  140.8 22.9 %copy-start.53 = (bf16[1,1,1,256,256]{3,4,2,1,0:T(8,128)(2,1)S(1)}, bf16[1,1,1,256,256]{3,4,2,1,0:T(8,128)(2,1)}, u32[]{:S(2)}) copy-start(bf16[1,1,1,256,256]{3,4,2,1,0:T(8,128)(2,1)} %copy.223) | copy-start | bytes 393220
  147.2 18.9 %copy-start.27 = (bf16[1,1,1,256,256]{3,4,2,1,0:T(8,128)(2,1)S(1)}, bf16[1,1,1,256,256]{3,4,2,1,0:T(8,128)(2,1)}, u32[]{:S(2)}) copy-start(bf16[1,1,1,256,256]{3,4,2,1,0:T(8,128)(2,1)} %copy.222) | copy-start | bytes 393220
  147.2 18.9 %copy-start.44 = (bf16[256,256]{1,0:T(8,128)(2,1)S(1)}, bf16[256,256]{1,0:T(8,128)(2,1)}, u32[]{:S(2)}) copy-start(bf16[256,256]{1,0:T(8,128)(2,1)} %bitcast_negate_fusion.4) | copy-start | bytes 393220
  155.1 13.5 %copy-start.29 = (bf16[1,1,1,256,256]{3,4,2,1,0:T(8,128)(2,1)S(1)}, bf16[1,1,1,256,256]{3,4,2,1,0:T(8,128)(2,1)}, u32[]{:S(2)}) copy-start(bf16[1,1,1,256,256]{3,4,2,1,0:T(8,128)(2,1)} %copy.204) | copy-start | bytes 393220
  155.1 13.5 %copy-start.52 = (bf16[256,256]{1,0:T(8,128)(2,1)S(1)}, bf16[256,256]{1,0:T(8,128)(2,1)}, u32[]{:S(2)}) copy-start(bf16[256,256]{1,0:T(8,128)(2,1)} %bitcast_negate_fusion.13) | copy-start | bytes 393220
  155.2 13.5 %copy-start.55 = (bf16[1,1,1,256,256]{3,4,2,1,0:T(8,128)(2,1)S(1)}, bf16[1,1,1,256,256]{3,4,2,1,0:T(8,128)(2,1)}, u32[]{:S(2)}) copy-start(bf16[1,1,1,256,256]{3,4,2,1,0:T(8,128)(2,1)} %copy.203) | copy-start | bytes 393220
  156.9 821.2 %collective-permute-start.3 = (bf16[6,1,32,512]{3,2,1,0:T(8,128)(2,1)}, bf16[6,1,32,512]{3,2,1,0:T(8,128)(2,1)}, u32[]{:S(2)}, u32[]{:S(2)}) collective-permute-start(bf16[6,1,32,512]{3,2,1,0:T(8,128)(2,1)} %get-tuple-element.82), channel_id=1, source_target_pairs={{1,0},{2,1},{3,2},{4,3},{5,4},{6,5},{7,6},{8,7},{9,8},{10,9},{11,1... | collective-permute-start | bytes 589832 | tf_op jit(solution)/shard_map/ppermute | solution.py:21
  163.7 817.5 %collective-permute-start.2 = (bf16[6,1,32,512]{3,2,1,0:T(8,128)(2,1)}, bf16[6,1,32,512]{3,2,1,0:T(8,128)(2,1)}, u32[]{:S(2)}, u32[]{:S(2)}) collective-permute-start(bf16[6,1,32,512]{3,2,1,0:T(8,128)(2,1)} %get-tuple-element.81), channel_id=1, source_target_pairs={{0,1},{1,2},{2,3},{3,4},{4,5},{5,6},{6,7},{7,8},{8,9},{9,10},{10,1... | collective-permute-start | bytes 589832 | tf_op jit(solution)/shard_map/ppermute | solution.py:19
  166.1 4.0 copy-start.28
  166.1 4.0 copy-start.50
  166.1 4.0 copy-start.54
  973.2 2.5 copy-start.1
  973.2 2.5 copy-start.9
  975.7 2.5 copy-start.26
  975.7 2.5 copy-start.39
  975.7 2.5 copy-start.51
  975.7 2.5 copy-start.69
  978.2 3.0 copy-start.25
  978.2 3.0 copy-start.38
  978.2 3.0 copy-start.48
  978.2 3.0 copy-start.67
  979.8 3.0 copy-start.23
  979.8 3.0 copy-start.36
  979.8 3.0 copy-start.47
  979.8 3.0 copy-start.66
  981.3 3.0 copy-start.22
  981.3 3.0 copy-start.35
  981.3 3.0 copy-start.46
  981.3 3.0 copy-start.65
  982.8 3.0 copy-start.21
  982.8 3.0 copy-start.34
  982.8 3.0 copy-start.45
  982.8 3.0 copy-start.64
  984.3 3.0 copy-start.19
  984.3 3.0 copy-start.32
  984.3 3.0 copy-start.43
  984.3 3.0 copy-start.63
  985.8 3.0 copy-start.17
  985.8 3.0 copy-start.31
  985.8 3.0 copy-start.42
  985.8 3.0 copy-start.62
  987.3 3.0 copy-start.15
  987.3 3.0 copy-start.30
  987.3 3.0 copy-start.40
  987.3 3.0 copy-start.61
  988.8 3.1 copy-start.20
  988.8 3.1 copy-start.33
  988.8 3.1 copy-start.41
  988.8 3.1 copy-start.60
  990.2 3.0 copy-start.2
  990.3 3.0 copy-start.3
  990.3 3.0 copy-start.6
  990.3 3.0 copy-start.7
  990.3 3.0 copy-start.11
  990.3 3.0 copy-start.13
  (11 other events, 17.0 us)
Sparse Core Ops, SparseCore 0:
  74.4 262.6 all-reduce.2
where the time goes:
time: 1010 us; the launch traced here: 1000 us
  blocking collectives  630 us (62%)
  waiting for transfers between devices  166 us (16%)
  local copies, waits for them, and re-layouts  102 us (10%)
  matrix products  41.5 us (4%)
  other arithmetic  40.3 us (4%)
  between operations  14.6 us (1%)
  starting transfers between devices  10.6 us (1%)
    all_gather x1, blocking collectives, local(): add_weighted = lax.all_gather(weighted, ('row', 'col'), axis=2, tiled=True)  630 us
    unnamed x2, waiting for transfers between devices  166 us
    unnamed x175, local copies, waits for them, and re-layouts  48.2 us
    dot_general x18, matrix products, local(): jnp.dot(block, near_mat, preferred_element_type=jnp.float32)  31.8 us
    neg x18, other arithmetic, realify(): lower = jnp.concatenate([-imag_part.T, real_part.T], axis=1)  21.7 us
  transfers between devices with their start and end apart: 5, of which 1 were waited for; matrix products, arithmetic and copies ran while one was open for 10% of the time, Pallas kernels for 0%

commit v1 on v0

--- a/solution.py
+++ b/solution.py
@@ -95,7 +95,10 @@
     count = owned.shape[2]
     scales = far_scale * lax.dynamic_slice_in_dim(wave_weight, owner * owned.shape[2], count, 0)
     weighted = (scales[None, None, :] * owned).astype(jnp.bfloat16)
-    add_weighted = lax.all_gather(weighted, ("row", "col"), axis=2, tiled=True)
+    add_weighted = jnp.concatenate(
+        lax.all_to_all(jnp.stack([weighted] * lax.axis_size(("row", "col"))), ("row", "col"), 0, 0),
+        axis=2,
+    )
     count = add_weighted.shape[2]
     cos_part = cos_all[:, None, :]
     sin_part = sin_all[:, None, :]

time: 1010 us -> 395 us (0.39)
  blocking collectives: 630 us -> 0 us
  starting transfers between devices: 10.6 us -> 22.9 us
  waiting for transfers between devices: 166 us -> 178 us
    all_gather x1 -> x0, blocking collectives: 630 us -> none  [local(): add_weighted = lax.all_gather(weighted, ('row', 'col'), axis=2, tiled=True)]
    unnamed x2, waiting for transfers between devices: 166 us -> 178 us
    all_to_all x0 -> x1, starting transfers between devices: none -> 12.3 us  [local(): lax.all_to_all(jnp.stack([weighted] * lax.axis_size(('row', 'col'))), ('r...]
    unnamed x175 -> x165, local copies, waits for them, and re-layouts: 48.2 us -> 43.1 us
  transfers between devices with their start and end apart: 5 -> 6, of which waited for: 1 -> 1; matrix products, arithmetic and copies ran while one was open for 10% -> 25% of each run, Pallas kernels for 0% -> 0%
where the time goes in v1:
time: 395 us; the launch traced here: 393 us
  waiting for transfers between devices  178 us (45%)
  local copies, waits for them, and re-layouts  95.7 us (24%)
  matrix products  44.3 us (11%)
  other arithmetic  37.2 us (9%)
  starting transfers between devices  22.9 us (6%)
  between operations  14.3 us (4%)
    unnamed x2, waiting for transfers between devices  178 us
    unnamed x165, local copies, waits for them, and re-layouts  43.1 us
    dot_general x18, matrix products, local(): jnp.dot(block, near_mat, preferred_element_type=jnp.float32)  34.6 us
    neg x18, other arithmetic, realify(): lower = jnp.concatenate([-imag_part.T, real_part.T], axis=1)  21 us
    all_to_all x1, starting transfers between devices, local(): lax.all_to_all(jnp.stack([weighted] * lax.axis_size(('row', 'col'))), ('r...  12.3 us
    slice x1, local copies, waits for them, and re-layouts, local(): projected[:, :, 1]  12.2 us
    reshape x1, local copies, waits for them, and re-layouts, local(): projected = projected.reshape(rows_here * cols_here, sources, 2, waves)  11.8 us
    ppermute x2, starting transfers between devices, extended(): lax.ppermute(head, axis, [((i + 1) % count, i) for i in range(count)])  10.6 us
  transfers between devices with their start and end apart: 6, of which 1 were waited for; matrix products, arithmetic and copies ran while one was open for 25% of the time, Pallas kernels for 0%

profile of v1, /device:TPU:0, one launch (start us, length us, event | category | flops | bytes accessed | tf_op | source)
XLA Modules:
  0.0 392.7 jit_solution(6565594236976592255)
XLA Ops:
  6.5 6.5 %fusion.185 = (bf16[2048,1,256]{2,1,0:T(2,128)(2,1)S(1)}, bf16[2048,1,256]{2,1,0:T(2,128)(2,1)}) fusion(bf16[2048,2,256]{2,1,0:T(2,128)(2,1)} %param.12), kind=kLoop, calls=%fused_computation.312 | loop fusion | bytes 4194304 | tf_op jit(solution)/shard_map/slice | solution.py:58
  13.0 5.8 %copy.241 = bf16[2048,1,256]{0,2,1:T(8,128)(2,1)} copy(bf16[2048,1,256]{2,1,0:T(2,128)(2,1)} %get-tuple-element.78) | data formatting | bytes 2097152
  18.8 2.6 copy.242
  21.6 1.1 copy-done.15
  22.6 7.4 %convolution_bitcast_fusion = f32[512,4096]{0,1:T(8,128)} fusion(bf16[512,512]{1,0:T(8,128)(2,1)} %bitcast.302, bf16[256,2048]{1,0:T(8,128)(2,1)} %bitcast.305, bf16[256,2048]{1,0:T(8,128)(2,1)S(1)} %bitcast_negate_fusion, bf16[256,2048]{1,0:T(8,128)(2,1)S(1)} %bitcast.298), kind=kOutput, calls=%fused_computation | convolution fusion | flops 2164260864 | bytes 12058624 | tf_op jit(solution)/shard_map/dot_general | solution.py:67
  30.0 9.0 %copy.192 = f32[512,4096]{1,0:T(8,128)} copy(f32[512,4096]{0,1:T(8,128)} %convolution_bitcast_fusion) | data formatting | bytes 16777216 | tf_op jit(solution)/shard_map/dot_general | solution.py:67
  38.9 11.8 %reshape.495 = f32[16,32,2,2048]{3,2,1,0:T(2,128)} reshape(f32[512,4096]{1,0:T(8,128)} %copy.192) | data formatting | bytes 16777216 | tf_op jit(solution)/shard_map/reshape | solution.py:68
  50.7 12.2 %fusion.182 = (f32[16,32,1,2048]{3,2,1,0:T(1,128)}, f32[16,32,1,2048]{3,2,1,0:T(1,128)}) fusion(f32[16,32,2,2048]{3,2,1,0:T(2,128)} %reshape.495), kind=kLoop, calls=%fused_computation.309 | loop fusion | bytes 16777216 | tf_op jit(solution)/shard_map/slice | solution.py:71
  65.8 6.9 %fusion.6 = (f32[2048,32]{0,1:T(8,128)S(1)}, f32[2048,32]{0,1:T(8,128)S(1)}, f32[2048,32]{0,1:T(8,128)S(1)}, f32[2048,32]{0,1:T(8,128)S(1)}) fusion(f32[16,32,1,2048]{3,2,1,0:T(1,128)} %get-tuple-element.38, f32[2048,16]{0,1:T(8,128)S(1)} %get-tuple-element.97, f32[2048,16]{0,1:T(8,128)S(1)} %get-tuple-element.96, f32[16,32,1,2048]{3,2,1,0:T(1,128)} %get-tuple-element.37), kind=kLoop, calls=%fused_computation.12 | loop fusion | flops 8126464 | bytes 9699328 | tf_op jit(solution)/shard_map/pw,psw->sw/dot_general | solution.py:70
  72.8 2.3 copy.193
  75.9 3.9 collective-permute-start.1
  79.7 2.7 fusion.183
  82.4 2.7 fusion.184
  85.1 1.7 fusion.180
  86.8 1.7 copy.274
  88.5 1.6 bitcast_negate_fusion.1
  90.1 1.7 copy.272
  91.7 1.6 bitcast_negate_fusion.2
  93.3 1.7 copy.270
  95.0 1.6 bitcast_negate_fusion.3
  96.5 1.7 copy.268
  98.2 1.6 bitcast_negate_fusion.4
  99.8 1.6 copy.266
  101.4 1.6 bitcast_negate_fusion.5
  103.0 1.7 copy.264
  104.7 1.6 bitcast_negate_fusion.6
  107.0 1.6 bitcast_negate_fusion.7
  110.2 1.0 copy.254
  111.9 1.0 copy.252
  113.6 1.6 copy.250
  115.2 1.6 bitcast_negate_fusion.13
  116.8 1.7 copy.248
  118.5 1.6 bitcast_negate_fusion.14
  120.8 1.6 bitcast_negate_fusion.15
  124.1 2.0 fusion.158
  126.1 2.5 fusion.85
  128.6 2.6 fusion.77
  142.8 1.4 compare_reduce_fusion.7
  144.2 0.9 constant_dynamic-update-slice_fusion.4
  145.4 1.0 constant_dynamic-update-slice_fusion.5
  147.1 6.7 %collective-permute-start.3 = (bf16[6,1,32,512]{3,2,1,0:T(8,128)(2,1)}, bf16[6,1,32,512]{3,2,1,0:T(8,128)(2,1)}, u32[]{:S(2)}, u32[]{:S(2)}) collective-permute-start(bf16[6,1,32,512]{3,2,1,0:T(8,128)(2,1)} %get-tuple-element.82), channel_id=1, source_target_pairs={{1,0},{2,1},{3,2},{4,3},{5,4},{6,5},{7,6},{8,7},{9,8},{10,9},{11,1... | collective-permute-start | bytes 589832 | tf_op jit(solution)/shard_map/ppermute | solution.py:21
  153.9 1.4 convolution_select_fusion
  155.3 1.5 convolution_select_fusion.1
  156.8 1.5 convolution_select_fusion.2
  158.3 1.4 convolution_select_fusion.3
  159.7 178.2 %all-reduce.3.cloned.1.call-done = f32[32,2,2048]{0,1,2:T(2,128)} async-done(((f32[32,2,2048]{0,1,2:T(2,128)}), f32[32,2,2048]{0,1,2:T(2,128)}) %all-reduce.3.cloned.1.call-update) | async-done | bytes 524304
  338.8 1.4 reshape.555
  340.2 12.3 %all-to-all-start = ((bf16[256,2,256]{2,1,0:T(2,128)(2,1)}), bf16[256,2,256]{2,1,0:T(2,128)(2,1)S(1)}, u32[]{:S(2)}, u32[]{:S(2)}) async-start(bf16[256,2,256]{2,1,0:T(2,128)(2,1)} %reshape.555), calls=%async_computation | async-start | bytes 524288 | tf_op jit(solution)/shard_map/all_to_all | solution.py:99
  352.6 2.6 convolution_select_fusion.4
  355.2 2.6 convolution_select_fusion.5
  357.8 2.4 convolution_select_fusion.6
  360.2 2.4 convolution_select_fusion.7
  362.7 2.4 convolution_select_fusion.8
  365.1 1.4 convolution_select_fusion.10
  366.5 1.4 convolution_select_fusion.11
  368.0 1.4 convolution_select_fusion.12
  369.4 1.5 convolution_select_fusion.13
  371.0 1.3 convolution_select_fusion.14
  372.4 1.7 fusion.26
  374.7 1.1 fusion.28
  375.8 1.5 copy.197
  377.7 2.4 add_convert_fusion
  380.3 2.4 fusion
  383.3 2.6 fusion.25
  (188 shorter events, 24.9 us)
Async XLA Ops:
  6.5 331.4 %all-reduce.3.cloned.1.call-start = ((), (), s32[]{:S(2)}) async-start(), calls=%async_computation.1 | async-start | bytes 4194304
  21.5 8.5 %copy-start = (bf16[2048,1,256]{0,2,1:T(8,128)(2,1)}, bf16[2048,1,256]{0,2,1:T(8,128)(2,1)S(1)}, u32[]{:S(2)}) copy-start(bf16[2048,1,256]{0,2,1:T(8,128)(2,1)S(1)} %copy.242) | copy-start | bytes 3145732
  50.7 12.9 %copy-start.60 = (s32[4,4,2]{1,2,0:T(2,128)S(1)}, s32[4,4,2]{1,2,0:T(2,128)}, u32[]{:S(2)}) copy-start(s32[4,4,2]{1,2,0:T(2,128)} %param.10) | copy-start | bytes 388
  50.7 14.3 %copy-start.59 = (s32[2048,2]{0,1:T(2,128)S(1)}, s32[2048,2]{0,1:T(2,128)}, u32[]{:S(2)}) copy-start(s32[2048,2]{0,1:T(2,128)} %param.11) | copy-start | bytes 49156
  75.9 68.4 %collective-permute-start = (bf16[1,4,32,512]{3,2,1,0:T(8,128)(2,1)}, bf16[1,4,32,512]{3,2,1,0:T(8,128)(2,1)}, u32[]{:S(2)}, u32[]{:S(2)}) collective-permute-start(bf16[1,4,32,512]{3,2,1,0:T(8,128)(2,1)} %get-tuple-element.89), channel_id=1, source_target_pairs={{0,16},{16,32},{32,48},{48,64},{64,80},{80,96},{96,112},{112,128},... | collective-permute-start | bytes 393224 | tf_op jit(solution)/shard_map/ppermute | solution.py:19
  75.9 69.5 %collective-permute-start.1 = (bf16[1,4,32,512]{3,2,1,0:T(8,128)(2,1)}, bf16[1,4,32,512]{3,2,1,0:T(8,128)(2,1)}, u32[]{:S(2)}, u32[]{:S(2)}) collective-permute-start(bf16[1,4,32,512]{3,2,1,0:T(8,128)(2,1)} %get-tuple-element.88), channel_id=1, source_target_pairs={{16,0},{32,16},{48,32},{64,48},{80,64},{96,80},{112,96},{128,112},... | collective-permute-start | bytes 393224 | tf_op jit(solution)/shard_map/ppermute | solution.py:21
  108.7 3.3 copy-start.25
  109.5 13.1 %copy-start.22 = (bf16[1,1,1,256,256]{3,4,2,1,0:T(8,128)(2,1)}, bf16[1,1,1,256,256]{3,4,2,1,0:T(8,128)(2,1)S(1)}, u32[]{:S(2)}) copy-start(bf16[1,1,1,256,256]{3,4,2,1,0:T(8,128)(2,1)S(1)} %copy.256) | copy-start | bytes 393220
  111.2 11.2 %copy-start.20 = (bf16[1,1,1,256,256]{3,4,2,1,0:T(8,128)(2,1)}, bf16[1,1,1,256,256]{3,4,2,1,0:T(8,128)(2,1)S(1)}, u32[]{:S(2)}) copy-start(bf16[1,1,1,256,256]{3,4,2,1,0:T(8,128)(2,1)S(1)} %copy.254) | copy-start | bytes 393220
  128.6 14.2 %copy-start.17 = (s32[4,4,9]{2,1,0:T(4,128)S(1)}, s32[4,4,9]{2,1,0:T(4,128)}, u32[]{:S(2)}) copy-start(s32[4,4,9]{2,1,0:T(4,128)} %param.9) | copy-start | bytes 1732
  131.2 22.6 %copy-start.33 = (bf16[1,1,1,256,256]{3,4,2,1,0:T(8,128)(2,1)S(1)}, bf16[1,1,1,256,256]{3,4,2,1,0:T(8,128)(2,1)}, u32[]{:S(2)}) copy-start(bf16[1,1,1,256,256]{3,4,2,1,0:T(8,128)(2,1)} %copy.270) | copy-start | bytes 393220
  131.2 22.6 %copy-start.45 = (bf16[256,256]{1,0:T(8,128)(2,1)S(1)}, bf16[256,256]{1,0:T(8,128)(2,1)}, u32[]{:S(2)}) copy-start(bf16[256,256]{1,0:T(8,128)(2,1)} %bitcast_negate_fusion.3) | copy-start | bytes 393220
  134.3 19.6 %copy-start.57 = (bf16[1,1,1,256,256]{3,4,2,1,0:T(8,128)(2,1)S(1)}, bf16[1,1,1,256,256]{3,4,2,1,0:T(8,128)(2,1)}, u32[]{:S(2)}) copy-start(bf16[1,1,1,256,256]{3,4,2,1,0:T(8,128)(2,1)} %copy.269) | copy-start | bytes 393220
  141.1 14.2 %copy-start.32 = (bf16[1,1,1,256,256]{3,4,2,1,0:T(8,128)(2,1)S(1)}, bf16[1,1,1,256,256]{3,4,2,1,0:T(8,128)(2,1)}, u32[]{:S(2)}) copy-start(bf16[1,1,1,256,256]{3,4,2,1,0:T(8,128)(2,1)} %copy.268) | copy-start | bytes 393220
  141.1 14.2 %copy-start.44 = (bf16[256,256]{1,0:T(8,128)(2,1)S(1)}, bf16[256,256]{1,0:T(8,128)(2,1)}, u32[]{:S(2)}) copy-start(bf16[256,256]{1,0:T(8,128)(2,1)} %bitcast_negate_fusion.4) | copy-start | bytes 393220
  141.1 14.2 %copy-start.56 = (bf16[1,1,1,256,256]{3,4,2,1,0:T(8,128)(2,1)S(1)}, bf16[1,1,1,256,256]{3,4,2,1,0:T(8,128)(2,1)}, u32[]{:S(2)}) copy-start(bf16[1,1,1,256,256]{3,4,2,1,0:T(8,128)(2,1)} %copy.267) | copy-start | bytes 393220
  145.4 11.4 %copy-start.35 = (bf16[1,1,1,256,256]{3,4,2,1,0:T(8,128)(2,1)S(1)}, bf16[1,1,1,256,256]{3,4,2,1,0:T(8,128)(2,1)}, u32[]{:S(2)}) copy-start(bf16[1,1,1,256,256]{3,4,2,1,0:T(8,128)(2,1)} %copy.250) | copy-start | bytes 393220
  145.4 11.4 %copy-start.52 = (bf16[256,256]{1,0:T(8,128)(2,1)S(1)}, bf16[256,256]{1,0:T(8,128)(2,1)}, u32[]{:S(2)}) copy-start(bf16[256,256]{1,0:T(8,128)(2,1)} %bitcast_negate_fusion.13) | copy-start | bytes 393220
  145.4 11.4 %copy-start.58 = (bf16[1,1,1,256,256]{3,4,2,1,0:T(8,128)(2,1)S(1)}, bf16[1,1,1,256,256]{3,4,2,1,0:T(8,128)(2,1)}, u32[]{:S(2)}) copy-start(bf16[1,1,1,256,256]{3,4,2,1,0:T(8,128)(2,1)} %copy.249) | copy-start | bytes 393220
  147.1 205.4 %collective-permute-start.3 = (bf16[6,1,32,512]{3,2,1,0:T(8,128)(2,1)}, bf16[6,1,32,512]{3,2,1,0:T(8,128)(2,1)}, u32[]{:S(2)}, u32[]{:S(2)}) collective-permute-start(bf16[6,1,32,512]{3,2,1,0:T(8,128)(2,1)} %get-tuple-element.82), channel_id=1, source_target_pairs={{1,0},{2,1},{3,2},{4,3},{5,4},{6,5},{7,6},{8,7},{9,8},{10,9},{11,1... | collective-permute-start | bytes 589832 | tf_op jit(solution)/shard_map/ppermute | solution.py:21
  153.8 203.9 %collective-permute-start.2 = (bf16[6,1,32,512]{3,2,1,0:T(8,128)(2,1)S(1)}, bf16[6,1,32,512]{3,2,1,0:T(8,128)(2,1)}, u32[]{:S(2)}, u32[]{:S(2)}) collective-permute-start(bf16[6,1,32,512]{3,2,1,0:T(8,128)(2,1)S(1)} %get-tuple-element.81), channel_id=1, source_target_pairs={{0,1},{1,2},{2,3},{3,4},{4,5},{5,6},{6,7},{7,8},{8,9},{9,10},{10,1... | collective-permute-start | bytes 589832 | tf_op jit(solution)/shard_map/ppermute | solution.py:19
  155.3 3.0 copy-start.34
  155.3 3.0 copy-start.50
  156.8 195.7 %copy-start.31 = (bf16[1,1,1,256,256]{3,4,2,1,0:T(8,128)(2,1)S(1)}, bf16[1,1,1,256,256]{3,4,2,1,0:T(8,128)(2,1)}, u32[]{:S(2)}) copy-start(bf16[1,1,1,256,256]{3,4,2,1,0:T(8,128)(2,1)} %copy.274) | copy-start | bytes 393220
  159.7 195.4 %copy-start.29 = (bf16[1,1,1,256,256]{3,4,2,1,0:T(8,128)(2,1)S(1)}, bf16[1,1,1,256,256]{3,4,2,1,0:T(8,128)(2,1)}, u32[]{:S(2)}) copy-start(bf16[1,1,1,256,256]{3,4,2,1,0:T(8,128)(2,1)} %copy.272) | copy-start | bytes 393220
  340.2 33.9 %all-to-all-start = ((bf16[256,2,256]{2,1,0:T(2,128)(2,1)}), bf16[256,2,256]{2,1,0:T(2,128)(2,1)S(1)}, u32[]{:S(2)}, u32[]{:S(2)}) async-start(bf16[256,2,256]{2,1,0:T(2,128)(2,1)} %reshape.555), calls=%async_computation | async-start | bytes 524288 | tf_op jit(solution)/shard_map/all_to_all | solution.py:99
  352.5 5.2 %copy-start.30 = (bf16[1,1,1,256,256]{3,4,2,1,0:T(8,128)(2,1)S(1)}, bf16[1,1,1,256,256]{3,4,2,1,0:T(8,128)(2,1)}, u32[]{:S(2)}) copy-start(bf16[1,1,1,256,256]{3,4,2,1,0:T(8,128)(2,1)} %copy.266) | copy-start | bytes 393220
  352.6 5.2 %copy-start.43 = (bf16[256,256]{1,0:T(8,128)(2,1)S(1)}, bf16[256,256]{1,0:T(8,128)(2,1)}, u32[]{:S(2)}) copy-start(bf16[256,256]{1,0:T(8,128)(2,1)} %bitcast_negate_fusion.5) | copy-start | bytes 393220
  352.6 5.2 %copy-start.55 = (bf16[1,1,1,256,256]{3,4,2,1,0:T(8,128)(2,1)S(1)}, bf16[1,1,1,256,256]{3,4,2,1,0:T(8,128)(2,1)}, u32[]{:S(2)}) copy-start(bf16[1,1,1,256,256]{3,4,2,1,0:T(8,128)(2,1)} %copy.265) | copy-start | bytes 393220
  355.1 5.0 %copy-start.28 = (bf16[1,1,1,256,256]{3,4,2,1,0:T(8,128)(2,1)S(1)}, bf16[1,1,1,256,256]{3,4,2,1,0:T(8,128)(2,1)}, u32[]{:S(2)}) copy-start(bf16[1,1,1,256,256]{3,4,2,1,0:T(8,128)(2,1)} %copy.264) | copy-start | bytes 393220
  355.2 5.0 %copy-start.42 = (bf16[256,256]{1,0:T(8,128)(2,1)S(1)}, bf16[256,256]{1,0:T(8,128)(2,1)}, u32[]{:S(2)}) copy-start(bf16[256,256]{1,0:T(8,128)(2,1)} %bitcast_negate_fusion.6) | copy-start | bytes 393220
  355.2 5.0 %copy-start.54 = (bf16[1,1,1,256,256]{3,4,2,1,0:T(8,128)(2,1)S(1)}, bf16[1,1,1,256,256]{3,4,2,1,0:T(8,128)(2,1)}, u32[]{:S(2)}) copy-start(bf16[1,1,1,256,256]{3,4,2,1,0:T(8,128)(2,1)} %copy.263) | copy-start | bytes 393220
  357.8 4.8 %copy-start.27 = (bf16[1,1,1,256,256]{3,4,2,1,0:T(8,128)(2,1)S(1)}, bf16[1,1,1,256,256]{3,4,2,1,0:T(8,128)(2,1)}, u32[]{:S(2)}) copy-start(bf16[1,1,1,256,256]{3,4,2,1,0:T(8,128)(2,1)} %copy.262) | copy-start | bytes 393220
  357.8 4.8 %copy-start.41 = (bf16[256,256]{1,0:T(8,128)(2,1)S(1)}, bf16[256,256]{1,0:T(8,128)(2,1)}, u32[]{:S(2)}) copy-start(bf16[256,256]{1,0:T(8,128)(2,1)} %bitcast_negate_fusion.7) | copy-start | bytes 393220
  357.8 4.8 %copy-start.53 = (bf16[1,1,1,256,256]{3,4,2,1,0:T(8,128)(2,1)S(1)}, bf16[1,1,1,256,256]{3,4,2,1,0:T(8,128)(2,1)}, u32[]{:S(2)}) copy-start(bf16[1,1,1,256,256]{3,4,2,1,0:T(8,128)(2,1)} %copy.261) | copy-start | bytes 393220
  360.2 4.9 %copy-start.26 = (bf16[1,1,1,256,256]{3,4,2,1,0:T(8,128)(2,1)S(1)}, bf16[1,1,1,256,256]{3,4,2,1,0:T(8,128)(2,1)}, u32[]{:S(2)}) copy-start(bf16[1,1,1,256,256]{3,4,2,1,0:T(8,128)(2,1)} %copy-done.25) | copy-start | bytes 393220
  360.2 4.8 %copy-start.40 = (bf16[256,256]{1,0:T(8,128)(2,1)S(1)}, bf16[256,256]{1,0:T(8,128)(2,1)}, u32[]{:S(2)}) copy-start(bf16[256,256]{1,0:T(8,128)(2,1)} %bitcast_negate_fusion.9) | copy-start | bytes 393220
  360.2 4.8 %copy-start.51 = (bf16[1,1,1,256,256]{3,4,2,1,0:T(8,128)(2,1)S(1)}, bf16[1,1,1,256,256]{3,4,2,1,0:T(8,128)(2,1)}, u32[]{:S(2)}) copy-start(bf16[1,1,1,256,256]{3,4,2,1,0:T(8,128)(2,1)} %copy.257) | copy-start | bytes 393220
  362.6 3.9 copy-start.23
  362.6 3.9 copy-start.38
  362.6 3.9 copy-start.49
  365.0 2.9 copy-start.21
  365.1 2.9 copy-start.37
  365.1 2.9 copy-start.48
  366.5 2.9 copy-start.36
  366.5 2.9 copy-start.46
  368.0 3.0 copy-start.24
  368.0 3.0 copy-start.39
  368.0 3.0 copy-start.47
  369.4 2.9 copy-start.4
  369.4 2.9 copy-start.5
  369.4 2.9 copy-start.11
  369.4 2.9 copy-start.13
  377.7 2.5 copy-start.1
  377.7 2.5 copy-start.3
  377.7 2.5 copy-start.16
  380.2 2.5 copy-start.6
  380.2 2.5 copy-start.7
  380.2 2.5 copy-start.8
  380.2 2.5 copy-start.10
  380.2 2.8 copy-start.12
  380.2 3.1 copy-start.14
  380.2 3.1 copy-start.18
  380.2 3.0 copy-start.19
  (5 other events, 7.1 us)
Sparse Core Ops, SparseCore 0:
  75.3 262.6 all-reduce.2
